TPU v7x, 128 devices: a whole 4x4x4 slice. The times are simulated.
128 devices in a mesh: samp: 32 (over x, y, core), var: 4 (over z).
Axes of the slice: x: 4, y: 4, z: 4, core: 2. Of those that a mesh axis runs over, the one named last changes fastest.
Arguments:
- genotypes: int32 [32768, 4096], P('samp', 'var'), may hold values from 0 to 2
- observed: int32 [32768, 4096], P('samp', 'var'), may hold values from 0 to 1, as said below
- proportions: float32 [10, 32768], P(None, 'samp'), may hold values from 0 to 1, as said below
- frequencies: float32 [10, 4096], P(None, ('samp', 'var')), may hold values from 0.02 to 0.98
Outputs:
- mixture: float32 [10, 32768], P(None, 'samp')
- alleles: float32 [10, 4096], P(None, 'var')
Inputs may be any that keep to these rules, and one draw needn't show every extreme that they name: Every sample is observed at 256 or more variants and every variant at 2048 or more samples. Each sample's 10 proportions are positive and sum to one.
All inputs are finite; a program needn't handle non-finite values.
Results may differ from a plain program's by a relative error of at most 0.0003.
Values sent between devices are 32-bit elements; how exact they have to be, the bound alone decides.
A program may use at most 128 MiB of HBM per device.

v0:
```python
import jax
import jax.numpy as jnp
from jax import lax
from jax.sharding import PartitionSpec as P

STEPS = 2
CLIP_LOW = 1e-05
NORM_EPS = 1e-10
EXACT = lax.Precision.HIGHEST


def clip_unit(values):
    return jnp.clip(values, CLIP_LOW, 1.0 - CLIP_LOW)


def tidy_mixture(mixture):
    clipped = clip_unit(mixture)
    return clipped / jnp.sum(clipped, axis=0, keepdims=True)


def step_size(first, second):
    return jnp.maximum(1.0, jnp.sqrt(first / (second + NORM_EPS)))


def allele_rule(alleles, alt_sums, ref_sums):
    weighted = alleles * alt_sums
    return clip_unit(weighted / (weighted + (1.0 - alleles) * ref_sums))


def local(genotypes, observed, proportions, frequencies):
    var_count = lax.axis_size("var")
    gathered = lax.all_gather(frequencies, ("samp", "var"), axis=1, tiled=True)
    owner_width = gathered.shape[1] // var_count
    alleles = lax.dynamic_slice_in_dim(
        gathered, lax.axis_index("var") * owner_width, owner_width, 1
    )
    seen_vals = observed.astype(jnp.float32)
    geno_vals = genotypes.astype(jnp.float32)
    alt_counts = seen_vals * geno_vals
    ref_counts = seen_vals * (2.0 - geno_vals)
    local_counts = jnp.sum(observed, axis=1).astype(jnp.float32)
    twice_observed = 2.0 * lax.psum(local_counts, "var")[None, :]

    def expectation_step(mixture, current):
        expected = lax.dot_general(
            mixture,
            current,
            (((0,), (0,)), ((), ())),
            precision=EXACT,
            preferred_element_type=jnp.float32,
        )
        ratio_alt = alt_counts / expected
        ratio_ref = ref_counts / (1.0 - expected)
        prop_terms = lax.dot_general(
            current,
            ratio_alt - ratio_ref,
            (((1,), (1,)), ((), ())),
            precision=EXACT,
            preferred_element_type=jnp.float32,
        )
        prop_terms = prop_terms + jnp.sum(ratio_ref, axis=1)[None, :]
        alt_terms = lax.dot_general(
            mixture,
            ratio_alt,
            (((1,), (0,)), ((), ())),
            precision=EXACT,
            preferred_element_type=jnp.float32,
        )
        ref_terms = lax.dot_general(
            mixture,
            ratio_ref,
            (((1,), (0,)), ((), ())),
            precision=EXACT,
            preferred_element_type=jnp.float32,
        )
        prop_sums = lax.psum(prop_terms, "var")
        next_mixture = clip_unit(mixture * prop_sums / twice_observed)
        alt_sums, ref_sums = lax.psum((alt_terms, ref_terms), "samp")
        next_alleles = allele_rule(current, alt_sums, ref_sums)
        return (next_mixture, next_alleles)

    mixture = proportions
    for repeat in range(STEPS):
        mixture_one, alleles_one = expectation_step(mixture, alleles)
        mixture_two, alleles_two = expectation_step(mixture_one, alleles_one)
        step_mix = mixture_one - mixture
        curve_mix = mixture_two - mixture_one - step_mix
        step_allele = alleles_one - alleles
        curve_allele = alleles_two - alleles_one - step_allele
        step_mix_local = jnp.sum(step_mix * step_mix)
        curve_mix_local = jnp.sum(curve_mix * curve_mix)
        step_allele_local = jnp.sum(step_allele * step_allele)
        curve_allele_local = jnp.sum(curve_allele * curve_allele)
        step_allele_sum, curve_allele_sum = lax.psum((step_allele_local, curve_allele_local), "var")
        step_mix_sum, curve_mix_sum = lax.psum((step_mix_local, curve_mix_local), "samp")
        alpha_mix = step_size(step_mix_sum, curve_mix_sum)
        alpha_allele = step_size(step_allele_sum, curve_allele_sum)
        extra_mix = tidy_mixture(
            mixture + 2.0 * alpha_mix * step_mix + alpha_mix * alpha_mix * curve_mix
        )
        extra_allele = clip_unit(
            alleles + 2.0 * alpha_allele * step_allele + alpha_allele * alpha_allele * curve_allele
        )
        mixture, alleles = expectation_step(extra_mix, extra_allele)
    return (mixture, alleles)


def solution(mesh):
    placed = (P("samp", "var"), P("samp", "var"), P(None, "samp"), P(None, ("samp", "var")))
    return jax.shard_map(
        local,
        mesh=mesh,
        in_specs=placed,
        out_specs=(P(None, "samp"), P(None, "var")),
        check_vma=False,
    )
```

profile of v0, /device:TPU:1, one launch (start us, length us, event | category | flops | bytes accessed | tf_op | source)
XLA Modules:
  0.0 985.0 jit_solution(3233084332891088129)
XLA Ops:
  7.2 0.0 all-reduce.22.cloned.1.call-start
  7.2 64.1 %all-gather = f32[128,32,10]{1,2,0:T(8,128)S(1)} all-gather(f32[1,32,10]{1,2,0:T(8,128)} %bitcast.70), channel_id=1, replica_groups=mesh['samp'=32,'var'=4] {'samp','var'}, dimensions={0}, use_global_device_ids=true | all-gather | bytes 165120 | tf_op jit(solution)/shard_map/all_gather | solution.py:32
  71.3 0.2 copy.12
  71.5 0.3 reshape.15
  71.8 5.4 copy.14
  77.2 5.4 copy.13
  82.6 12.0 %fusion.78 = (f32[1024]{0:T(1024)S(1)}, f32[1024,1024]{0,1:T(8,128)S(1)}, f32[1024,1024]{0,1:T(8,128)}, f32[1024,1024]{0,1:T(8,128)S(1)}, f32[1024,1024]{1,0:T(8,128)S(1)}) fusion(s32[1024,1024]{0,1:T(8,128)} %copy.14, s32[1024,1024]{0,1:T(8,128)} %copy.13, f32[10,1024]{1,0:T(8,128)S(1)} %copy-done.11, f32[4096,10]{0,1:T(8,128)S(1)} %reshape.15, ...), kind=kOutput, calls=%fused_computation.104 | convolution fusion | flops 134216704 | bytes 25300996 | tf_op jit(solution)/shard_map/dot_general | solution.py:45
  94.6 2.0 copy-done
  96.5 4.3 convolution_bitcast_fusion
  100.8 4.7 convolution_bitcast_fusion.1
  105.5 10.7 %all-reduce.20.cloned.1.call-start = ((), (), s32[]{:S(2)}) async-start(), calls=%async_computation.2 | async-start | bytes 262144 | tf_op jit(solution)/shard_map/psum | solution.py:78
  116.2 2.5 reduce_sum.154
  118.6 7.4 fusion.13
  126.0 13.1 %all-reduce.8 = (f32[10,1024]{1,0:T(8,128)S(1)}, f32[1024]{0:T(1024)S(1)}) all-reduce(f32[10,1024]{1,0:T(8,128)S(1)} %fusion.13, f32[1024]{0:T(1024)S(1)} %convert_element_type.11), channel_id=1, replica_groups=mesh['samp'=32,'var'=4] {'var'}, use_global_device_ids=true, to_apply=%region_1.0 | all-reduce | flops 11264 | bytes 90112 | tf_op jit(solution)/shard_map/psum | solution.py:76
  139.2 65.9 %all-reduce.22.cloned.1.call-done = (f32[10,1024]{1,0:T(8,128)}, f32[10,1024]{1,0:T(8,128)}) async-done(((f32[10,1024]{1,0:T(8,128)}, f32[10,1024]{1,0:T(8,128)}), (f32[10,1024]{1,0:T(8,128)}, f32[10,1024]{1,0:T(8,128)})) %all-reduce.22.cloned.1.call-update) | async-done | bytes 81936 | tf_op jit(solution)/shard_map/psum | solution.py:78
  205.1 1.5 multiply_reduce_fusion.5
  206.6 9.0 fusion.77
  215.6 3.5 fusion.65
  219.2 3.5 fusion.80
  222.7 2.7 fusion.16
  225.4 14.0 %psum.194 = f32[10,1024]{1,0:T(8,128)S(1)} all-reduce(f32[10,1024]{1,0:T(8,128)S(1)} %fusion.16), channel_id=1, replica_groups=mesh['samp'=32,'var'=4] {'var'}, use_global_device_ids=true, to_apply=%region_9.10 | all-reduce | flops 10240 | bytes 81920 | tf_op jit(solution)/shard_map/psum | solution.py:76
  239.4 0.6 multiply_reduce_fusion.6
  240.0 125.1 %all-reduce.23 = (f32[10,1024]{1,0:T(8,128)S(1)}, f32[10,1024]{1,0:T(8,128)S(1)}, f32[]{:T(128)}, f32[]{:T(128)}) all-reduce(f32[10,1024]{1,0:T(8,128)S(1)} %fusion.80, f32[10,1024]{1,0:T(8,128)S(1)} %fusion.65, f32[]{:T(128)} %get-tuple-element.5, f32[]{:T(128)} %get-tuple-element.4), channel_id=1, replica_groups=mesh['samp'=32,'var'=4] {'samp'}, use_global_device_ids=true, to_apply=%region_16.17 | all-reduce | flops 20482 | bytes 163856 | tf_op jit(solution)/shard_map/psum | solution.py:78
  366.4 0.6 multiply_reduce_fusion.4
  367.0 7.0 all-reduce.7
  375.4 0.1 fusion.74
  375.5 9.0 fusion.73
  384.5 4.2 fusion.50
  388.7 4.2 fusion.49
  392.9 7.3 fusion.19
  400.3 12.7 %psum.200 = f32[10,1024]{1,0:T(8,128)S(1)} all-reduce(f32[10,1024]{1,0:T(8,128)S(1)} %fusion.19), channel_id=1, replica_groups=mesh['samp'=32,'var'=4] {'var'}, use_global_device_ids=true, to_apply=%region_20.21 | all-reduce | flops 10240 | bytes 81920 | tf_op jit(solution)/shard_map/psum | solution.py:76
  413.0 0.0 all-reduce.20.cloned.1.call-update
  413.0 0.2 all-reduce.18.cloned.1.call-start
  413.3 106.5 %all-reduce.20.cloned.1.call-done = (f32[10,1024]{1,0:T(8,128)}, f32[10,1024]{1,0:T(8,128)}) async-done(((f32[10,1024]{1,0:T(8,128)}, f32[10,1024]{1,0:T(8,128)}), (f32[10,1024]{1,0:T(8,128)}, f32[10,1024]{1,0:T(8,128)})) %all-reduce.20.cloned.1.call-update) | async-done | bytes 81936 | tf_op jit(solution)/shard_map/psum | solution.py:78
  519.8 0.9 fusion.35
  520.7 9.0 fusion.72
  529.7 4.2 fusion.60
  533.9 4.2 fusion.81
  538.1 7.3 fusion.22
  545.4 13.9 %psum.203 = f32[10,1024]{1,0:T(8,128)S(1)} all-reduce(f32[10,1024]{1,0:T(8,128)S(1)} %fusion.22), channel_id=1, replica_groups=mesh['samp'=32,'var'=4] {'var'}, use_global_device_ids=true, to_apply=%region_24.25 | all-reduce | flops 10240 | bytes 81920 | tf_op jit(solution)/shard_map/psum | solution.py:76
  559.4 0.0 all-reduce.18.cloned.1.call-update
  559.4 0.3 all-reduce.16.cloned.1.call-start
  559.7 102.3 %all-reduce.18.cloned.1.call-done = (f32[10,1024]{1,0:T(8,128)}, f32[10,1024]{1,0:T(8,128)}) async-done(((f32[10,1024]{1,0:T(8,128)}, f32[10,1024]{1,0:T(8,128)}), (f32[10,1024]{1,0:T(8,128)}, f32[10,1024]{1,0:T(8,128)})) %all-reduce.18.cloned.1.call-update) | async-done | bytes 81936 | tf_op jit(solution)/shard_map/psum | solution.py:78
  662.1 0.9 fusion.36
  663.0 9.0 fusion.71
  672.0 3.5 fusion.57
  675.5 3.5 fusion.82
  679.1 2.7 fusion.25
  681.7 13.9 %psum.207 = f32[10,1024]{1,0:T(8,128)S(1)} all-reduce(f32[10,1024]{1,0:T(8,128)S(1)} %fusion.25), channel_id=1, replica_groups=mesh['samp'=32,'var'=4] {'var'}, use_global_device_ids=true, to_apply=%region_30.31 | all-reduce | flops 10240 | bytes 81920 | tf_op jit(solution)/shard_map/psum | solution.py:76
  695.7 0.6 multiply_reduce_fusion.2
  696.3 125.1 %all-reduce.24 = (f32[10,1024]{1,0:T(8,128)S(1)}, f32[10,1024]{1,0:T(8,128)S(1)}, f32[]{:T(128)}, f32[]{:T(128)}) all-reduce(f32[10,1024]{1,0:T(8,128)S(1)} %fusion.82, f32[10,1024]{1,0:T(8,128)S(1)} %fusion.57, f32[]{:T(128)} %get-tuple-element.3, f32[]{:T(128)} %get-tuple-element.2), channel_id=1, replica_groups=mesh['samp'=32,'var'=4] {'samp'}, use_global_device_ids=true, to_apply=%region_37.38 | all-reduce | flops 20482 | bytes 163856 | tf_op jit(solution)/shard_map/psum | solution.py:78
  822.8 0.6 multiply_reduce_fusion
  823.4 0.6 multiply_reduce_fusion.1
  824.0 6.9 all-reduce.6
  832.2 0.1 fusion.69
  832.3 9.0 fusion.68
  841.4 4.2 fusion.53
  845.6 4.2 fusion.52
  849.8 7.3 fusion.28
  857.1 12.7 %psum.213 = f32[10,1024]{1,0:T(8,128)S(1)} all-reduce(f32[10,1024]{1,0:T(8,128)S(1)} %fusion.28), channel_id=1, replica_groups=mesh['samp'=32,'var'=4] {'var'}, use_global_device_ids=true, to_apply=%region_41.42 | all-reduce | flops 10240 | bytes 81920 | tf_op jit(solution)/shard_map/psum | solution.py:76
  869.8 0.0 all-reduce.16.cloned.1.call-update
  869.9 0.7 divide_clamp_fusion
  870.5 106.0 %all-reduce.16.cloned.1.call-done = (f32[10,1024]{1,0:T(8,128)}, f32[10,1024]{1,0:T(8,128)}) async-done(((f32[10,1024]{1,0:T(8,128)}, f32[10,1024]{1,0:T(8,128)}), (f32[10,1024]{1,0:T(8,128)}, f32[10,1024]{1,0:T(8,128)})) %all-reduce.16.cloned.1.call-update) | async-done | bytes 81936 | tf_op jit(solution)/shard_map/psum | solution.py:78
  976.5 1.5 fusion.40
  (36 shorter events, 0.2 us)
Async XLA Ops:
  7.2 197.9 %all-reduce.22.cloned.1.call-start = ((), (), s32[]{:S(2)}) async-start(), calls=%async_computation.3 | async-start | bytes 262144 | tf_op jit(solution)/shard_map/psum | solution.py:78
  77.2 5.4 copy-start.11
  94.6 2.0 copy-start
  94.6 6.2 copy-start.4
  94.6 6.2 copy-start.10
  105.5 414.3 %all-reduce.20.cloned.1.call-start = ((), (), s32[]{:S(2)}) async-start(), calls=%async_computation.2 | async-start | bytes 262144 | tf_op jit(solution)/shard_map/psum | solution.py:78
  206.6 9.0 copy-start.5
  375.5 9.1 copy-start.6
  384.5 4.2 copy-start.13
  384.5 4.2 copy-start.2
  413.0 249.0 %all-reduce.18.cloned.1.call-start = ((), (), s32[]{:S(2)}) async-start(), calls=%async_computation.1 | async-start | bytes 262144 | tf_op jit(solution)/shard_map/psum | solution.py:78
  520.7 9.1 copy-start.7
  529.7 4.2 copy-start.14
  529.7 4.2 copy-start.3
  559.4 417.1 %all-reduce.16.cloned.1.call-start = ((), (), s32[]{:S(2)}) async-start(), calls=%async_computation | async-start | bytes 262144 | tf_op jit(solution)/shard_map/psum | solution.py:78
  663.0 9.0 copy-start.8
  832.3 9.1 copy-start.9
  841.4 4.2 copy-start.12
  841.4 4.2 copy-start.1
Sparse Core Ops, SparseCore 0:
  105.6 99.4 all-reduce.21
  413.2 106.5 all-reduce.19
  559.5 102.4 all-reduce.17
  870.0 106.4 all-reduce.15
where the time goes:
time: 994 us; the launch traced here: 985 us
  blocking collectives  409 us (41%)
  waiting for transfers between devices  381 us (38%)
  matrix products  140 us (14%)
  between operations  19.9 us (2%)
  local copies, waits for them, and re-layouts  13.3 us (1%)
  other arithmetic  11.3 us (1%)
  starting transfers between devices  11.2 us (1%)
    psum x4, waiting for transfers between devices, expectation_step(): alt_sums, ref_sums = lax.psum((alt_terms, ref_terms), 'samp')  381 us
    psum x2, blocking collectives, expectation_step(): alt_sums, ref_sums = lax.psum((alt_terms, ref_terms), 'samp')  250 us
    psum x6, blocking collectives, expectation_step(): prop_sums = lax.psum(prop_terms, 'var')  80.4 us
    all_gather x1, blocking collectives, local(): gathered = lax.all_gather(frequencies, ('samp', 'var'), axis=1, tiled=True)  64.1 us
    dot_general x6, matrix products, expectation_step(): lax.dot_general(mixture, current, (((0,), (0,)), ((), ())), precision=EXA...  57.1 us
    dot_general x6, matrix products, expectation_step(): lax.dot_general(current, ratio_alt - ratio_ref, (((1,), (1,)), ((), ())),...  34.7 us
    dot_general x6, matrix products, expectation_step(): lax.dot_general(mixture, ratio_alt, (((1,), (0,)), ((), ())), precision=E...  24.2 us
    dot_general x6, matrix products, expectation_step(): lax.dot_general(mixture, ratio_ref, (((1,), (0,)), ((), ())), precision=E...  24 us
  transfers between devices with their start and end apart: 4, of which 4 were waited for; matrix products, arithmetic and copies ran while one was open for 1% of the time, Pallas kernels for 0%

commit v1 on v0

--- a/solution.py
+++ b/solution.py
@@ -73,7 +73,7 @@
             precision=EXACT,
             preferred_element_type=jnp.float32,
         )
-        prop_sums = lax.psum(prop_terms, "var")
+        prop_sums = jnp.sum(lax.all_gather(prop_terms, "var"), axis=0)
         next_mixture = clip_unit(mixture * prop_sums / twice_observed)
         alt_sums, ref_sums = lax.psum((alt_terms, ref_terms), "samp")
         next_alleles = allele_rule(current, alt_sums, ref_sums)

time: 994 us -> 978 us (0.984)
  blocking collectives: 409 us -> 399 us
    psum x6 -> x1, blocking collectives: 80.4 us -> 7.43 us  [local(): twice_observed = 2.0 * lax.psum(local_counts, 'var')[None, :]]
    all_gather x0 -> x6, blocking collectives: none -> 59.6 us  [expectation_step(): prop_sums = jnp.sum(lax.all_gather(prop_terms, 'var'), axis=0)]
where the time goes in v1:
time: 978 us; the launch traced here: 969 us
  blocking collectives  399 us (41%)
  waiting for transfers between devices  375 us (38%)
  matrix products  140 us (14%)
  between operations  19.8 us (2%)
  local copies, waits for them, and re-layouts  13.3 us (1%)
  other arithmetic  11.5 us (1%)
  starting transfers between devices  11 us (1%)
    psum x4, waiting for transfers between devices, expectation_step(): alt_sums, ref_sums = lax.psum((alt_terms, ref_terms), 'samp')  374 us
    psum x2, blocking collectives, expectation_step(): alt_sums, ref_sums = lax.psum((alt_terms, ref_terms), 'samp')  249 us
    all_gather x1, blocking collectives, local(): gathered = lax.all_gather(frequencies, ('samp', 'var'), axis=1, tiled=True)  64.1 us
    all_gather x6, blocking collectives, expectation_step(): prop_sums = jnp.sum(lax.all_gather(prop_terms, 'var'), axis=0)  59.6 us
    dot_general x6, matrix products, expectation_step(): lax.dot_general(mixture, current, (((0,), (0,)), ((), ())), precision=EXA...  57.1 us
    dot_general x6, matrix products, expectation_step(): lax.dot_general(current, ratio_alt - ratio_ref, (((1,), (1,)), ((), ())),...  34.7 us
    dot_general x6, matrix products, expectation_step(): lax.dot_general(mixture, ratio_alt, (((1,), (0,)), ((), ())), precision=E...  24.2 us
    dot_general x6, matrix products, expectation_step(): lax.dot_general(mixture, ratio_ref, (((1,), (0,)), ((), ())), precision=E...  24 us
  transfers between devices with their start and end apart: 4, of which 4 were waited for; matrix products, arithmetic and copies ran while one was open for 1% of the time, Pallas kernels for 0%

profile of v1, /device:TPU:1, one launch (start us, length us, event | category | flops | bytes accessed | tf_op | source)
XLA Modules:
  0.0 968.6 jit_solution(5159945845993591590)
XLA Ops:
  7.2 0.0 all-reduce.21.cloned.1.call-start
  7.2 64.1 %all-gather.6 = f32[128,32,10]{1,2,0:T(8,128)S(1)} all-gather(f32[1,32,10]{1,2,0:T(8,128)} %bitcast.82), channel_id=1, replica_groups=mesh['samp'=32,'var'=4] {'samp','var'}, dimensions={0}, use_global_device_ids=true | all-gather | bytes 165120 | tf_op jit(solution)/shard_map/all_gather | solution.py:32
  71.3 0.2 copy.12
  71.5 0.3 reshape.21
  71.8 5.4 copy.14
  77.2 5.4 copy.13
  82.6 12.0 %fusion.96 = (f32[1024]{0:T(1024)S(1)}, f32[1024,1024]{0,1:T(8,128)S(1)}, f32[1024,1024]{0,1:T(8,128)}, f32[1024,1024]{0,1:T(8,128)S(1)}, f32[1024,1024]{1,0:T(8,128)S(1)}) fusion(s32[1024,1024]{0,1:T(8,128)} %copy.14, s32[1024,1024]{0,1:T(8,128)} %copy.13, f32[10,1024]{1,0:T(8,128)S(1)} %copy-done.11, f32[4096,10]{0,1:T(8,128)S(1)} %reshape.21, ...), kind=kOutput, calls=%fused_computation.110 | convolution fusion | flops 134216704 | bytes 25300996 | tf_op jit(solution)/shard_map/dot_general | solution.py:45
  94.6 2.0 copy-done
  96.5 4.3 convolution_bitcast_fusion
  100.8 4.7 convolution_bitcast_fusion.1
  105.5 10.5 %all-reduce.19.cloned.1.call-start = ((), (), s32[]{:S(2)}) async-start(), calls=%async_computation.2 | async-start | bytes 262144 | tf_op jit(solution)/shard_map/psum | solution.py:78
  116.0 2.5 reduce_sum.209
  118.5 7.4 psum.147
  125.9 7.3 fusion.16
  133.3 9.8 %all-gather.7 = f32[4,10,1024]{2,1,0:T(8,128)S(1)} all-gather(f32[1,10,1024]{2,1,0:T(8,128)S(1)} %fusion.16), channel_id=2, replica_groups=mesh['samp'=32,'var'=4] {'var'}, dimensions={0}, use_global_device_ids=true | all-gather | bytes 204800 | tf_op jit(solution)/shard_map/all_gather | solution.py:76
  143.1 62.0 %all-reduce.21.cloned.1.call-done = (f32[10,1024]{1,0:T(8,128)}, f32[10,1024]{1,0:T(8,128)}) async-done(((f32[10,1024]{1,0:T(8,128)}, f32[10,1024]{1,0:T(8,128)}), (f32[10,1024]{1,0:T(8,128)}, f32[10,1024]{1,0:T(8,128)})) %all-reduce.21.cloned.1.call-update) | async-done | bytes 81936 | tf_op jit(solution)/shard_map/psum | solution.py:78
  205.1 1.5 multiply_reduce_fusion.5
  206.6 9.0 fusion.95
  215.6 3.5 fusion.83
  219.2 3.5 fusion.98
  222.7 2.7 fusion.22
  225.4 10.4 %all-gather.8 = f32[4,10,1024]{2,1,0:T(8,128)S(1)} all-gather(f32[1,10,1024]{2,1,0:T(8,128)S(1)} %fusion.22), channel_id=3, replica_groups=mesh['samp'=32,'var'=4] {'var'}, dimensions={0}, use_global_device_ids=true | all-gather | bytes 204800 | tf_op jit(solution)/shard_map/all_gather | solution.py:76
  235.8 0.6 multiply_reduce_fusion.6
  236.4 124.6 %all-reduce.22 = (f32[10,1024]{1,0:T(8,128)S(1)}, f32[10,1024]{1,0:T(8,128)S(1)}, f32[]{:T(128)}, f32[]{:T(128)}) all-reduce(f32[10,1024]{1,0:T(8,128)S(1)} %fusion.98, f32[10,1024]{1,0:T(8,128)S(1)} %fusion.83, f32[]{:T(128)} %get-tuple-element.5, f32[]{:T(128)} %get-tuple-element.4), channel_id=1, replica_groups=mesh['samp'=32,'var'=4] {'samp'}, use_global_device_ids=true, to_apply=%region_16.17 | all-reduce | flops 20482 | bytes 163856 | tf_op jit(solution)/shard_map/psum | solution.py:78
  362.3 0.6 multiply_reduce_fusion.4
  362.9 9.2 all-reduce.7
  373.5 0.1 fusion.92
  373.6 9.0 fusion.91
  382.6 4.2 fusion.68
  386.8 4.2 fusion.67
  391.0 7.3 fusion.28
  398.4 9.4 all-gather.9
  407.7 0.0 all-reduce.19.cloned.1.call-update
  407.8 0.2 all-reduce.17.cloned.1.call-start
  408.0 105.5 %all-reduce.19.cloned.1.call-done = (f32[10,1024]{1,0:T(8,128)}, f32[10,1024]{1,0:T(8,128)}) async-done(((f32[10,1024]{1,0:T(8,128)}, f32[10,1024]{1,0:T(8,128)}), (f32[10,1024]{1,0:T(8,128)}, f32[10,1024]{1,0:T(8,128)})) %all-reduce.19.cloned.1.call-update) | async-done | bytes 81936 | tf_op jit(solution)/shard_map/psum | solution.py:78
  513.5 0.9 fusion.53
  514.4 9.0 fusion.90
  523.5 4.2 fusion.78
  527.7 4.2 fusion.99
  531.9 7.3 fusion.34
  539.2 10.4 %all-gather.10 = f32[4,10,1024]{2,1,0:T(8,128)S(1)} all-gather(f32[1,10,1024]{2,1,0:T(8,128)S(1)} %fusion.34), channel_id=5, replica_groups=mesh['samp'=32,'var'=4] {'var'}, dimensions={0}, use_global_device_ids=true | all-gather | bytes 204800 | tf_op jit(solution)/shard_map/all_gather | solution.py:76
  549.6 0.0 all-reduce.17.cloned.1.call-update
  549.6 0.3 all-reduce.15.cloned.1.call-start
  549.9 101.9 %all-reduce.17.cloned.1.call-done = (f32[10,1024]{1,0:T(8,128)}, f32[10,1024]{1,0:T(8,128)}) async-done(((f32[10,1024]{1,0:T(8,128)}, f32[10,1024]{1,0:T(8,128)}), (f32[10,1024]{1,0:T(8,128)}, f32[10,1024]{1,0:T(8,128)})) %all-reduce.17.cloned.1.call-update) | async-done | bytes 81936 | tf_op jit(solution)/shard_map/psum | solution.py:78
  651.8 0.9 fusion.54
  652.7 9.0 fusion.89
  661.7 3.5 fusion.75
  665.2 3.5 fusion.100
  668.8 2.7 fusion.40
  671.5 10.4 %all-gather.11 = f32[4,10,1024]{2,1,0:T(8,128)S(1)} all-gather(f32[1,10,1024]{2,1,0:T(8,128)S(1)} %fusion.40), channel_id=6, replica_groups=mesh['samp'=32,'var'=4] {'var'}, dimensions={0}, use_global_device_ids=true | all-gather | bytes 204800 | tf_op jit(solution)/shard_map/all_gather | solution.py:76
  681.9 0.6 multiply_reduce_fusion.2
  682.5 124.6 %all-reduce.23 = (f32[10,1024]{1,0:T(8,128)S(1)}, f32[10,1024]{1,0:T(8,128)S(1)}, f32[]{:T(128)}, f32[]{:T(128)}) all-reduce(f32[10,1024]{1,0:T(8,128)S(1)} %fusion.100, f32[10,1024]{1,0:T(8,128)S(1)} %fusion.75, f32[]{:T(128)} %get-tuple-element.3, f32[]{:T(128)} %get-tuple-element.2), channel_id=1, replica_groups=mesh['samp'=32,'var'=4] {'samp'}, use_global_device_ids=true, to_apply=%region_37.38 | all-reduce | flops 20482 | bytes 163856 | tf_op jit(solution)/shard_map/psum | solution.py:78
  808.4 0.6 multiply_reduce_fusion
  809.1 0.6 multiply_reduce_fusion.1
  809.7 9.0 all-reduce.6
  820.1 0.1 fusion.87
  820.2 9.0 fusion.86
  829.2 4.2 fusion.71
  833.4 4.2 fusion.70
  837.6 7.3 fusion.46
  844.9 9.4 all-gather.12
  854.3 0.7 divide_clamp_fusion
  855.0 105.1 %all-reduce.15.cloned.1.call-done = (f32[10,1024]{1,0:T(8,128)}, f32[10,1024]{1,0:T(8,128)}) async-done(((f32[10,1024]{1,0:T(8,128)}, f32[10,1024]{1,0:T(8,128)}), (f32[10,1024]{1,0:T(8,128)}, f32[10,1024]{1,0:T(8,128)})) %all-reduce.15.cloned.1.call-update) | async-done | bytes 81936 | tf_op jit(solution)/shard_map/psum | solution.py:78
  960.1 1.5 fusion.58
  (43 shorter events, 0.3 us)
Async XLA Ops:
  7.2 197.9 %all-reduce.21.cloned.1.call-start = ((), (), s32[]{:S(2)}) async-start(), calls=%async_computation.3 | async-start | bytes 262144 | tf_op jit(solution)/shard_map/psum | solution.py:78
  77.2 5.4 copy-start.11
  94.6 2.0 copy-start
  94.6 6.2 copy-start.4
  94.6 6.2 copy-start.10
  105.5 408.0 %all-reduce.19.cloned.1.call-start = ((), (), s32[]{:S(2)}) async-start(), calls=%async_computation.2 | async-start | bytes 262144 | tf_op jit(solution)/shard_map/psum | solution.py:78
  206.6 9.0 copy-start.5
  373.6 9.1 copy-start.6
  382.6 4.2 copy-start.13
  382.6 4.2 copy-start.2
  407.8 244.0 %all-reduce.17.cloned.1.call-start = ((), (), s32[]{:S(2)}) async-start(), calls=%async_computation.1 | async-start | bytes 262144 | tf_op jit(solution)/shard_map/psum | solution.py:78
  514.4 9.1 copy-start.7
  523.5 4.2 copy-start.14
  523.5 4.2 copy-start.3
  549.6 410.5 %all-reduce.15.cloned.1.call-start = ((), (), s32[]{:S(2)}) async-start(), calls=%async_computation | async-start | bytes 262144 | tf_op jit(solution)/shard_map/psum | solution.py:78
  652.7 9.0 copy-start.8
  820.2 9.1 copy-start.9
  829.2 4.2 copy-start.12
  829.2 4.2 copy-start.1
Sparse Core Ops, SparseCore 0:
  105.6 99.4 all-reduce.20
  407.9 105.5 all-reduce.18
  549.7 102.0 all-reduce.16
  854.5 105.5 all-reduce.14
